TPU v7x, 512 devices: a whole 4x8x8 slice. The times are simulated.
512 devices in a mesh: section: 8 (over x, core), dp: 64 (over z, y).
Axes of the slice: x: 4, y: 8, z: 8, core: 2. Of those that a mesh axis runs over, the one named last changes fastest.
Arguments:
- inputs: bfloat16 [8, 1024, 4096], P(None, 'dp')
- cotangent: bfloat16 [8, 1024, 4096], P(None, 'dp'), may hold values from -0.59765625 to 0.59765625
- row_adapter_slot: int32 [8, 1024], P(None, 'dp'), may hold values from 0 to 1
- deployed_adapter_ids: int32 [64, 2], replicated, may hold values from 0 to 63, as said below
- adapter_owner_device: int32 [64], replicated, may hold values from 0 to 63, each once
- adapter_down_weight: bfloat16 [8, 1, 64, 2, 32, 4096], P('section', None, 'dp'), as said below
- adapter_up_weight: bfloat16 [8, 1, 64, 2, 32, 4096], P('section', None, 'dp'), as said below
Outputs:
- grad_down: float32 [8, 1, 64, 32, 4096], P('section', None, 'dp')
- grad_up: float32 [8, 1, 64, 32, 4096], P('section', None, 'dp')
Inputs may be any that keep to these rules, and one draw needn't show every extreme that they name: `deployed_adapter_ids`: the 2 adapter ids of one device differ, and every adapter is deployed on at least one device; some adapters are deployed on many devices. `adapter_owner_device`: every data device owns exactly one adapter. `adapter_down_weight`: copies of the same adapter on different devices are equal. `adapter_up_weight`: copies of the same adapter on different devices are equal.
All inputs are finite; a program needn't handle non-finite values.
Results may differ from a plain program's by a relative error of at most 0.0086.
Values may be sent and summed in bfloat16 or wider, within the bound.
A program may use at most 64 MiB of HBM per device.

v0:
```python
import jax
import jax.numpy as jnp
from jax import lax
from jax.sharding import PartitionSpec as P

adapter_scale = 0.5
epsilon = 1e-06


def from_behind(block, axis, distance):
    devices = range(lax.axis_size(axis))
    route = [(i - distance, i) for i in devices if i - distance in devices]
    return lax.ppermute(block, axis, route)


def norm_parts(hidden_state):
    value_rows = hidden_state.astype(jnp.float32)
    inverse = lax.rsqrt(jnp.mean(value_rows * value_rows, axis=-1, keepdims=True) + epsilon)
    return (inverse, value_rows * inverse)


def layer_forward(hidden_state, down_weight, up_weight, row_mask):
    inverse, unit = norm_parts(hidden_state)
    normed = unit.astype(jnp.bfloat16)
    rank_complete = lax.dot_general(
        normed, down_weight, (((1,), (1,)), ((), ())), preferred_element_type=jnp.float32
    )
    rank_row_values = jnp.where(row_mask, rank_complete, 0.0).astype(jnp.bfloat16)
    row_updates = jnp.dot(rank_row_values, up_weight, preferred_element_type=jnp.float32)
    return (
        (hidden_state.astype(jnp.float32) + adapter_scale * row_updates).astype(jnp.bfloat16),
        rank_row_values,
    )


def layer_backward(hidden_state, grad_rows, down_weight, up_weight, row_mask):
    inverse, unit = norm_parts(hidden_state)
    normed = unit.astype(jnp.bfloat16)
    rank_complete = adapter_scale * lax.dot_general(
        grad_rows, up_weight, (((1,), (1,)), ((), ())), preferred_element_type=jnp.float32
    )
    rank_grads = jnp.where(row_mask, rank_complete, 0.0).astype(jnp.bfloat16)
    unit_grads = jnp.dot(rank_grads, down_weight, preferred_element_type=jnp.float32)
    back_rows = grad_rows.astype(jnp.float32) + inverse * (
        unit_grads - unit * jnp.mean(unit_grads * unit, axis=-1, keepdims=True)
    )
    return (back_rows.astype(jnp.bfloat16), normed, rank_grads)


def put_block(store, layer_idx, position, value, usable):
    previous = store[layer_idx, position]
    return store.at[layer_idx, position].set(jnp.where(usable, value, previous))


def body(
    inputs,
    cotangent,
    row_adapter_slot,
    deployed_adapter_ids,
    adapter_owner_device,
    adapter_down_weight,
    adapter_up_weight,
):
    sections = lax.axis_size("section")
    section_index = lax.axis_index("section")
    pieces = lax.axis_size("dp")
    micro_count, row_count, feature_rows = inputs.shape
    layer_stack = adapter_down_weight.shape[1]
    adapter_slot_count = adapter_down_weight.shape[3]
    rank_length = adapter_down_weight.shape[4]
    rank_columns = adapter_slot_count * rank_length
    piece_cols = feature_rows // pieces
    down_weight = adapter_down_weight.reshape(layer_stack, rank_columns, feature_rows)
    up_weight = adapter_up_weight.reshape(layer_stack, rank_columns, feature_rows)
    column_slot = jnp.arange(rank_columns, dtype=jnp.int32) // rank_length
    masks = row_adapter_slot[..., None] == column_slot
    step_count = micro_count + sections - 1
    ticks = jnp.arange(step_count, dtype=jnp.int32)

    def forward_tick(carried, tick_now):
        incoming, saved_in, saved_rank = carried
        micro_index = tick_now - section_index
        usable = (micro_index >= 0) & (micro_index < micro_count)
        position = jnp.clip(micro_index, 0, micro_count - 1)
        hidden_state = jnp.where(section_index == 0, inputs[position], incoming)
        row_mask = masks[position]
        saved_in = put_block(saved_in, 0, position, hidden_state, usable)
        hidden_state, rank_row_values = layer_forward(
            hidden_state, down_weight[0], up_weight[0], row_mask
        )
        saved_rank = put_block(saved_rank, 0, position, rank_row_values, usable)
        incoming = from_behind(hidden_state, "section", 1)
        return ((incoming, saved_in, saved_rank), None)

    start_forward = (
        jnp.zeros((row_count, feature_rows), jnp.bfloat16),
        jnp.zeros((layer_stack, micro_count, row_count, feature_rows), jnp.bfloat16),
        jnp.zeros((layer_stack, micro_count, row_count, rank_columns), jnp.bfloat16),
    )
    (unused_rows, saved_in, saved_rank), unused_out = lax.scan(forward_tick, start_forward, ticks)
    records = (
        jnp.zeros((layer_stack, micro_count, row_count, feature_rows), jnp.bfloat16),
        jnp.zeros((layer_stack, micro_count, row_count, rank_columns), jnp.bfloat16),
    )

    def backward_tick(carried, tick_now):
        incoming, records = carried
        micro_index = tick_now - (sections - 1 - section_index)
        usable = (micro_index >= 0) & (micro_index < micro_count)
        position = jnp.clip(micro_index, 0, micro_count - 1)
        grad_rows = jnp.where(section_index == sections - 1, cotangent[position], incoming)
        row_mask = masks[position]
        for layer_idx in reversed(range(layer_stack)):
            hidden_state = saved_in[layer_idx, position]
            rank_row_values = saved_rank[layer_idx, position]
            back_rows, normed, rank_grads = layer_backward(
                hidden_state, grad_rows, down_weight[layer_idx], up_weight[layer_idx], row_mask
            )
            records = (
                put_block(records[0], layer_idx, position, grad_rows, usable),
                put_block(records[1], layer_idx, position, rank_grads, usable),
            )
            grad_rows = back_rows
        incoming = from_behind(grad_rows, "section", -1)
        return ((incoming, records), None)

    start_backward = (jnp.zeros((row_count, feature_rows), jnp.bfloat16), records)
    (unused_grads, records), unused_out = lax.scan(backward_tick, start_backward, ticks)
    token_count = micro_count * row_count
    normed_all = (
        norm_parts(saved_in)[1]
        .astype(jnp.bfloat16)
        .reshape(layer_stack, token_count, pieces, piece_cols)
    )
    grads_all = records[0].reshape(layer_stack, token_count, pieces, piece_cols)
    normed_recv, grads_recv = (
        lax.all_to_all(normed_all, "dp", split_axis=2, concat_axis=1, tiled=True),
        lax.all_to_all(grads_all, "dp", split_axis=2, concat_axis=1, tiled=True),
    )
    normed_recv = normed_recv.reshape(layer_stack, pieces, token_count, piece_cols)
    grads_recv = grads_recv.reshape(layer_stack, pieces, token_count, piece_cols)
    rank_local = saved_rank.reshape(layer_stack, token_count, rank_columns)
    rank_grad_local = records[1].reshape(layer_stack, token_count, rank_columns)
    rank_every, rank_grad_every = (
        lax.all_gather(rank_local, "dp", axis=1, tiled=True),
        lax.all_gather(rank_grad_local, "dp", axis=1, tiled=True),
    )
    rank_every = rank_every.reshape(layer_stack, pieces, token_count, rank_columns)
    rank_grad_every = rank_grad_every.reshape(layer_stack, pieces, token_count, rank_columns)
    pieces_down = jnp.einsum(
        "lstk,lstc->slkc", rank_grad_every, normed_recv, preferred_element_type=jnp.float32
    )
    up_gradient_pieces = adapter_scale * jnp.einsum(
        "lstk,lstc->slkc", rank_every, grads_recv, preferred_element_type=jnp.float32
    )
    pieces_down = pieces_down.reshape(
        pieces, layer_stack, adapter_slot_count, rank_length * piece_cols
    )
    up_gradient_pieces = up_gradient_pieces.reshape(
        pieces, layer_stack, adapter_slot_count, rank_length * piece_cols
    )
    adapters = adapter_owner_device.shape[0]
    adapter_ids = jnp.arange(adapters, dtype=jnp.int32)
    owner_of = jnp.sum(
        jnp.where(deployed_adapter_ids[..., None] == adapter_ids, adapter_owner_device, 0), axis=-1
    )
    owner_ids = jnp.arange(pieces, dtype=jnp.int32)
    select = (owner_of[None, :, :] == owner_ids[:, None, None]).astype(jnp.float32)
    owned_down = jnp.einsum("osk,slkx->olx", select, pieces_down, precision=lax.Precision.HIGHEST)
    owned_up = jnp.einsum(
        "osk,slkx->olx", select, up_gradient_pieces, precision=lax.Precision.HIGHEST
    )
    owned_down = owned_down.reshape(pieces, layer_stack, rank_length, piece_cols)
    owned_up = owned_up.reshape(pieces, layer_stack, rank_length, piece_cols)
    final_down, final_up = (
        lax.all_to_all(
            owned_down.astype(jnp.bfloat16), "dp", split_axis=0, concat_axis=3, tiled=True
        ).astype(owned_down.dtype),
        lax.all_to_all(
            owned_up.astype(jnp.bfloat16), "dp", split_axis=0, concat_axis=3, tiled=True
        ).astype(owned_up.dtype),
    )
    grad_down = final_down.reshape(1, layer_stack, 1, rank_length, feature_rows)
    grad_up = final_up.reshape(1, layer_stack, 1, rank_length, feature_rows)
    return (grad_down, grad_up)


def solution(mesh):
    placed = (
        P(None, "dp", None),
        P(None, "dp", None),
        P(None, "dp"),
        P(),
        P(),
        P("section", None, "dp", None, None, None),
        P("section", None, "dp", None, None, None),
    )
    return jax.shard_map(
        body,
        mesh=mesh,
        in_specs=placed,
        out_specs=(P("section", None, "dp", None, None), P("section", None, "dp", None, None)),
        check_vma=False,
    )
```

profile of v0, /device:TPU:4, one launch (start us, length us, event | category | flops | bytes accessed | tf_op | source)
XLA Modules:
  0.0 656.7 jit_solution(1103574373725658941)
XLA Ops:
  8.2 210.0 %while.35 = (s32[]{:T(128)}, bf16[16,4096]{1,0:T(8,128)(2,1)S(1)}, bf16[1,8,16,4096]{3,2,1,0:T(8,128)(2,1)S(1)}, bf16[1,8,16,64]{3,2,1,0:T(8,128)(2,1)S(1)}, pre...) while((s32[]{:T(128)}, bf16[16,4096]{1,0:T(8,128)(2,1)S(1)}, ...), condition=%wide.region_4.5_spmd, body=%wide.region_1.4_spmd.sunk | while | flops 17633332 | bytes 3036152 | solution.py:100
  17.8 4.4 collective-permute-done
  31.8 4.4 collective-permute-done
  45.8 4.4 collective-permute-done
  59.8 4.4 collective-permute-done
  73.8 4.4 collective-permute-done
  87.8 4.4 collective-permute-done
  101.8 4.4 collective-permute-done
  115.8 4.4 collective-permute-done
  129.8 4.4 collective-permute-done
  143.8 4.4 collective-permute-done
  157.8 4.4 collective-permute-done
  171.8 4.4 collective-permute-done
  185.8 4.4 collective-permute-done
  199.8 4.4 collective-permute-done
  213.8 4.4 collective-permute-done
  218.3 192.8 %while.36 = (s32[]{:T(128)}, bf16[16,4096]{1,0:T(8,128)(2,1)S(1)}, bf16[1,8,16,4096]{3,2,1,0:T(8,128)(2,1)S(1)}, bf16[1,8,16,64]{3,2,1,0:T(8,128)(2,1)S(1)}, pre...) while((s32[]{:T(128)}, bf16[16,4096]{1,0:T(8,128)(2,1)S(1)}, ...), condition=%wide.region_9.10_spmd, body=%wide.region_5.9_spmd.sunk | while | flops 17962036 | bytes 5919656 | solution.py:128
  236.1 3.8 collective-permute-start.1
  249.1 3.8 collective-permute-start.1
  262.1 3.8 collective-permute-start.1
  288.0 3.8 collective-permute-start.1
  301.0 3.8 collective-permute-start.1
  314.0 3.8 collective-permute-start.1
  339.9 3.8 collective-permute-start.1
  419.6 16.9 %all-to-all-start = ((bf16[1,128,64,64]{1,3,0,2:T(8,128)(2,1)}), bf16[1,128,64,64]{1,3,0,2:T(8,128)(2,1)}, u32[]{:S(2)}, u32[]{:S(2)}) async-start(bf16[1,128,64,64]{1,3,0,2:T(8,128)(2,1)} %copy.52), calls=%async_computation | async-start | bytes 2097152 | tf_op jit(solution)/shard_map/all_to_all | solution.py:137
  442.5 24.9 %all-to-all-done = bf16[1,128,64,64]{1,3,0,2:T(8,128)(2,1)} async-done(((bf16[1,128,64,64]{1,3,0,2:T(8,128)(2,1)}), bf16[1,128,64,64]{1,3,0,2:T(8,128)(2,1)}, u32[]{:S(2)}, u32[]{:S(2)}) %all-to-all-start) | async-done | bytes 1048608 | tf_op jit(solution)/shard_map/all_to_all | solution.py:137
  467.4 8.2 %all-to-all-start.2 = ((bf16[1,128,64,64]{1,3,0,2:T(8,128)(2,1)}), bf16[1,128,64,64]{1,3,0,2:T(8,128)(2,1)}, u32[]{:S(2)}, u32[]{:S(2)}) async-start(bf16[1,128,64,64]{1,3,0,2:T(8,128)(2,1)} %copy.59), calls=%async_computation.2 | async-start | bytes 2097152 | tf_op jit(solution)/shard_map/all_to_all | solution.py:138
  475.8 46.8 %all-gather.3.cloned.1.call-done = bf16[1,8192,64]{1,2,0:T(8,128)(2,1)} async-done(((bf16[1,128,64]{1,2,0:T(8,128)(2,1)}), bf16[1,8192,64]{1,2,0:T(8,128)(2,1)}) %all-gather.3.cloned.1.call-update) | async-done | bytes 1048592 | tf_op jit(solution)/shard_map/all_gather | solution.py:146
  534.6 67.2 %all-gather.5.cloned.1.call-done = bf16[1,8192,64]{1,2,0:T(8,128)(2,1)} async-done(((bf16[1,128,64]{1,2,0:T(8,128)(2,1)}), bf16[1,8192,64]{1,2,0:T(8,128)(2,1)}) %all-gather.5.cloned.1.call-update) | async-done | bytes 1048592 | tf_op jit(solution)/shard_map/all_gather | solution.py:145
  603.2 8.0 %all-to-all-start.1 = ((bf16[64,2,1024]{2,1,0:T(2,128)(2,1)}), bf16[64,2,1024]{2,1,0:T(2,128)(2,1)S(1)}, u32[]{:S(2)}, u32[]{:S(2)}) async-start(bf16[64,2,1024]{2,1,0:T(2,128)(2,1)} %reshape.335), calls=%async_computation.1 | async-start | bytes 524288 | tf_op jit(solution)/shard_map/all_to_all | solution.py:176
  624.6 9.5 %all-to-all-start.3 = ((bf16[64,2,1024]{2,1,0:T(2,128)(2,1)}), bf16[64,2,1024]{2,1,0:T(2,128)(2,1)S(1)}, u32[]{:S(2)}, u32[]{:S(2)}) async-start(bf16[64,2,1024]{2,1,0:T(2,128)(2,1)} %reshape.337), calls=%async_computation.3 | async-start | bytes 524288 | tf_op jit(solution)/shard_map/all_to_all | solution.py:179
  636.3 11.3 %all-to-all-done.3 = bf16[64,2,1024]{2,1,0:T(2,128)(2,1)S(1)} async-done(((bf16[64,2,1024]{2,1,0:T(2,128)(2,1)}), bf16[64,2,1024]{2,1,0:T(2,128)(2,1)S(1)}, u32[]{:S(2)}, u32[]{:S(2)}) %all-to-all-start.3) | async-done | bytes 262176 | tf_op jit(solution)/shard_map/all_to_all | solution.py:179
  (422 shorter events, 337.0 us)
Async XLA Ops:
  7.2 515.4 %all-gather.3.cloned.1.call-start = ((), (), s32[]{:S(2)}) async-start(), calls=%async_computation.4 | async-start | bytes 1064960 | tf_op jit(solution)/shard_map/all_gather | solution.py:146
  15.9 6.3 collective-permute-start
  29.9 6.3 collective-permute-start
  43.9 6.3 collective-permute-start
  57.9 6.3 collective-permute-start
  71.9 6.3 collective-permute-start
  85.9 6.3 collective-permute-start
  99.9 6.3 collective-permute-start
  113.9 6.3 collective-permute-start
  127.9 6.3 collective-permute-start
  141.9 6.3 collective-permute-start
  155.9 6.3 collective-permute-start
  169.9 6.3 collective-permute-start
  183.9 6.3 collective-permute-start
  236.1 6.3 collective-permute-start.1
  249.1 6.3 collective-permute-start.1
  262.1 6.3 collective-permute-start.1
  275.0 6.3 collective-permute-start.1
  288.0 6.3 collective-permute-start.1
  301.0 6.3 collective-permute-start.1
  314.0 6.3 collective-permute-start.1
  326.9 6.3 collective-permute-start.1
  339.9 6.3 collective-permute-start.1
  365.9 6.3 collective-permute-start.1
  378.8 6.3 collective-permute-start.1
  391.8 6.3 collective-permute-start.1
  404.8 6.3 collective-permute-start.1
  419.6 47.8 %all-to-all-start = ((bf16[1,128,64,64]{1,3,0,2:T(8,128)(2,1)}), bf16[1,128,64,64]{1,3,0,2:T(8,128)(2,1)}, u32[]{:S(2)}, u32[]{:S(2)}) async-start(bf16[1,128,64,64]{1,3,0,2:T(8,128)(2,1)} %copy.52), calls=%async_computation | async-start | bytes 2097152 | tf_op jit(solution)/shard_map/all_to_all | solution.py:137
  436.5 165.2 %all-gather.5.cloned.1.call-start = ((), (), s32[]{:S(2)}) async-start(), calls=%async_computation.5 | async-start | bytes 1064960 | tf_op jit(solution)/shard_map/all_gather | solution.py:145
  467.4 135.8 %all-to-all-start.2 = ((bf16[1,128,64,64]{1,3,0,2:T(8,128)(2,1)}), bf16[1,128,64,64]{1,3,0,2:T(8,128)(2,1)}, u32[]{:S(2)}, u32[]{:S(2)}) async-start(bf16[1,128,64,64]{1,3,0,2:T(8,128)(2,1)} %copy.59), calls=%async_computation.2 | async-start | bytes 2097152 | tf_op jit(solution)/shard_map/all_to_all | solution.py:138
  603.2 21.4 %all-to-all-start.1 = ((bf16[64,2,1024]{2,1,0:T(2,128)(2,1)}), bf16[64,2,1024]{2,1,0:T(2,128)(2,1)S(1)}, u32[]{:S(2)}, u32[]{:S(2)}) async-start(bf16[64,2,1024]{2,1,0:T(2,128)(2,1)} %reshape.335), calls=%async_computation.1 | async-start | bytes 524288 | tf_op jit(solution)/shard_map/all_to_all | solution.py:176
  624.6 23.1 %all-to-all-start.3 = ((bf16[64,2,1024]{2,1,0:T(2,128)(2,1)}), bf16[64,2,1024]{2,1,0:T(2,128)(2,1)S(1)}, u32[]{:S(2)}, u32[]{:S(2)}) async-start(bf16[64,2,1024]{2,1,0:T(2,128)(2,1)} %reshape.337), calls=%async_computation.3 | async-start | bytes 524288 | tf_op jit(solution)/shard_map/all_to_all | solution.py:179
  (21 other events, 188.7 us)
Sparse Core Ops, SparseCore 0:
  411.9 110.5 all-gather.2
  526.1 75.5 all-gather.4
where the time goes:
time: 662 us; the launch traced here: 657 us
  waiting for transfers between devices  256 us (39%)
  starting transfers between devices  126 us (19%)
  other arithmetic  98.3 us (15%)
  matrix products  89.6 us (14%)
  local copies, waits for them, and re-layouts  51.3 us (8%)
  loops' own time  21 us (3%)
  between operations  14.3 us (2%)
    ppermute x30, waiting for transfers between devices, from_behind(): return lax.ppermute(block, axis, route)  103 us
    ppermute x30, starting transfers between devices, from_behind(): return lax.ppermute(block, axis, route)  83.6 us
    all_gather x1, waiting for transfers between devices, body(): lax.all_gather(rank_local, 'dp', axis=1, tiled=True)  67.2 us
    scatter x30, other arithmetic, put_block(): return store.at[layer_idx, position].set(jnp.where(usable, value, previous))  47 us
    all_gather x1, waiting for transfers between devices, body(): lax.all_gather(rank_grad_local, 'dp', axis=1, tiled=True)  46.8 us
    another operation x30, other arithmetic  41.5 us
    dot_general x15, matrix products, layer_forward(): lax.dot_general(normed, down_weight, (((1,), (1,)), ((), ())), preferred_...  29.6 us
    dot_general x15, matrix products, layer_backward(): lax.dot_general(grad_rows, up_weight, (((1,), (1,)), ((), ())), preferred...  27.9 us
  transfers between devices with their start and end apart: 36, of which 35 were waited for; matrix products, arithmetic and copies ran while one was open for 6% of the time, Pallas kernels for 0%

commit v1 on v0

v1 whole, which is shorter than its diff:
```python
import jax
import jax.numpy as jnp
from jax import lax
from jax.experimental import pallas as pl
from jax.experimental.pallas import tpu as pltpu
from jax.sharding import PartitionSpec as P

adapter_scale = 0.5
epsilon = 1e-06


def relay_kernel(x_ref, c_ref, slot_ref, down_ref, up_ref, out_ref, hidden_ref, grad_ref):
    sections, rank_columns, width = down_ref.shape
    rows = x_ref.shape[0]
    half = rank_columns // 2
    column_slot = lax.broadcasted_iota(jnp.int32, (rows, rank_columns), 1) // half
    row_mask = slot_ref[...] == column_slot
    hidden_ref[0] = x_ref[...]
    grad_ref[...] = c_ref[...]

    def norm_parts(section):
        hidden = hidden_ref[section].astype(jnp.float32)
        inverse = lax.rsqrt(jnp.mean(hidden * hidden, axis=-1, keepdims=True) + epsilon)
        return hidden, inverse, hidden * inverse

    def forward(section, carried):
        hidden, inverse, unit = norm_parts(section)
        normed = unit.astype(jnp.bfloat16)
        out_ref[section, :, 0:width] = normed
        rank = lax.dot_general(
            normed,
            down_ref[section],
            (((1,), (1,)), ((), ())),
            preferred_element_type=jnp.float32,
        )
        rank = jnp.where(row_mask, rank, 0.0).astype(jnp.bfloat16)
        out_ref[section, :, 2 * width : 2 * width + rank_columns] = rank
        update = jnp.dot(rank, up_ref[section], preferred_element_type=jnp.float32)
        hidden_ref[section + 1] = (hidden + adapter_scale * update).astype(jnp.bfloat16)
        return carried

    lax.fori_loop(0, sections, forward, 0)

    def backward(step, carried):
        section = sections - 1 - step
        hidden, inverse, unit = norm_parts(section)
        grads = grad_ref[...]
        out_ref[section, :, width : 2 * width] = grads
        rank_grads = adapter_scale * lax.dot_general(
            grads,
            up_ref[section],
            (((1,), (1,)), ((), ())),
            preferred_element_type=jnp.float32,
        )
        rank_grads = jnp.where(row_mask, rank_grads, 0.0).astype(jnp.bfloat16)
        out_ref[section, :, 2 * width + 128 : 2 * width + 128 + rank_columns] = rank_grads
        unit_grads = jnp.dot(rank_grads, down_ref[section], preferred_element_type=jnp.float32)
        back = grads.astype(jnp.float32) + inverse * (
            unit_grads - unit * jnp.mean(unit_grads * unit, axis=-1, keepdims=True)
        )
        grad_ref[...] = back.astype(jnp.bfloat16)
        return carried

    lax.fori_loop(0, sections, backward, 0)


def relay(x, c, slot, down_every, up_every):
    sections, rank_columns, width = down_every.shape
    rows = x.shape[0]
    vmem = pl.BlockSpec(memory_space=pltpu.VMEM)
    return pl.pallas_call(
        relay_kernel,
        out_shape=jax.ShapeDtypeStruct((sections, rows, 2 * width + 256), jnp.bfloat16),
        in_specs=[vmem] * 5,
        out_specs=vmem,
        scratch_shapes=[
            pltpu.VMEM((sections + 1, rows, width), jnp.bfloat16),
            pltpu.VMEM((rows, width), jnp.bfloat16),
        ],
        compiler_params=pltpu.CompilerParams(vmem_limit_bytes=48 * 1024 * 1024),
    )(x, c, slot, down_every, up_every)


def body(
    inputs,
    cotangent,
    row_adapter_slot,
    deployed_adapter_ids,
    adapter_owner_device,
    adapter_down_weight,
    adapter_up_weight,
):
    section_index = lax.axis_index("section")
    pieces = lax.axis_size("dp")
    micro_count, row_count, width = inputs.shape
    slot_count = adapter_down_weight.shape[3]
    rank = adapter_down_weight.shape[4]
    rank_columns = slot_count * rank
    down_every = lax.all_gather(adapter_down_weight.reshape(rank_columns, width), "section")
    up_every = lax.all_gather(adapter_up_weight.reshape(rank_columns, width), "section")
    x = lax.dynamic_index_in_dim(inputs, section_index, 0, keepdims=False)
    c = lax.dynamic_index_in_dim(cotangent, section_index, 0, keepdims=False)
    slot = lax.dynamic_index_in_dim(row_adapter_slot, section_index, 0, keepdims=False)
    packed = relay(x, c, slot[:, None], down_every, up_every)
    packed = lax.all_to_all(packed, "section", split_axis=0, concat_axis=0, tiled=True)
    packed = packed.reshape(micro_count * row_count, 2 * width + 256)
    normed = packed[:, :width]
    grads = packed[:, width : 2 * width]
    rank_rows = packed[:, 2 * width : 2 * width + rank_columns]
    rank_grads = packed[:, 2 * width + 128 : 2 * width + 128 + rank_columns]

    def tile(rank_values, row_values):
        return jnp.concatenate(
            [
                lax.dot_general(
                    rank_values[:, k * rank : (k + 1) * rank],
                    row_values,
                    (((0,), (0,)), ((), ())),
                    preferred_element_type=jnp.float32,
                )
                for k in range(slot_count)
            ],
            axis=-1,
        )

    tiles = jnp.concatenate(
        [tile(rank_grads, normed), adapter_scale * tile(rank_rows, grads)], axis=0
    ).astype(jnp.bfloat16)
    lanes = width // 128
    tiles = tiles.reshape(pieces, slot_count * lanes, 128)
    tiles = lax.all_to_all(tiles, "dp", split_axis=0, concat_axis=0, tiled=True)
    tiles = tiles.reshape(pieces, slot_count, width)
    adapter_ids = jnp.arange(adapter_owner_device.shape[0], dtype=jnp.int32)
    owner_of = jnp.sum(
        jnp.where(deployed_adapter_ids[..., None] == adapter_ids, adapter_owner_device, 0), axis=-1
    )
    owner_ids = jnp.arange(pieces, dtype=jnp.int32)
    select = (owner_of[None, :, :] == owner_ids[:, None, None]).astype(jnp.bfloat16)
    owned = jnp.einsum("odk,dkx->ox", select, tiles, preferred_element_type=jnp.float32)
    owned = owned.astype(jnp.bfloat16).reshape(pieces, lanes, 128)
    final = lax.all_to_all(owned, "dp", split_axis=0, concat_axis=0, tiled=True)
    final = final.reshape(2, 1, 1, 1, rank, width).astype(jnp.float32)
    return (final[0], final[1])


def solution(mesh):
    placed = (
        P(None, "dp", None),
        P(None, "dp", None),
        P(None, "dp"),
        P(),
        P(),
        P("section", None, "dp", None, None, None),
        P("section", None, "dp", None, None, None),
    )
    return jax.shard_map(
        body,
        mesh=mesh,
        in_specs=placed,
        out_specs=(P("section", None, "dp", None, None), P("section", None, "dp", None, None)),
        check_vma=False,
    )
```

time: 662 us -> 218 us (0.33)
  the two profiles are of different devices: /device:TPU:4 before, /device:TPU:8 now
where the time goes in v1:
time: 218 us
  waiting for transfers between devices  112 us (51%)
  blocking collectives  56 us (26%)
  Pallas kernels  14.6 us (7%)
  between operations  14.2 us (7%)
  starting transfers between devices  13.5 us (6%)
  local copies, waits for them, and re-layouts  3.67 us (2%)
  matrix products  2.66 us (1%)
    all_gather x1, waiting for transfers between devices, body(): lax.all_gather(adapter_down_weight.reshape(rank_columns, width), 'section')  42.3 us
    all_gather x1, waiting for transfers between devices, body(): lax.all_gather(adapter_up_weight.reshape(rank_columns, width), 'section')  39.6 us
    all_to_all x1, blocking collectives, body(): lax.all_to_all(packed, 'section', split_axis=0, concat_axis=0, tiled=True)  30.7 us
    all_to_all x1, waiting for transfers between devices, body(): tiles = lax.all_to_all(tiles, 'dp', split_axis=0, concat_axis=0, tiled=True)  29 us
    all_to_all x1, blocking collectives, body(): final = lax.all_to_all(owned, 'dp', split_axis=0, concat_axis=0, tiled=True)  25.3 us
    pallas_call x1, Pallas kernels, relay(): pl.pallas_call(relay_kernel, out_shape=jax.ShapeDtypeStruct((sections, ro...  14.6 us
    all_to_all x1, starting transfers between devices, body(): tiles = lax.all_to_all(tiles, 'dp', split_axis=0, concat_axis=0, tiled=True)  13.4 us
  transfers between devices with their start and end apart: 3, of which 3 were waited for; matrix products, arithmetic and copies ran while one was open for 1% of the time, Pallas kernels for 0%

profile of v1, /device:TPU:8, one launch (start us, length us, event | category | flops | bytes accessed | tf_op | source)
XLA Modules:
  0.0 218.2 jit_solution(15422846043117757954)
XLA Ops:
  7.2 0.0 copy-start
  7.2 0.0 all-gather.3.cloned.1.call-start
  7.2 0.7 all-gather.3.cloned.1.call-update
  7.9 0.0 all-gather.5.cloned.1.call-start
  8.0 0.7 all-gather.5.cloned.1.call-update
  8.7 0.1 copy.17.slot_ref
  8.8 1.0 dynamic-slice_bitcast_fusion
  9.8 42.3 %all-gather.3.cloned.1.call-done.down_ref = bf16[8,64,4096]{2,1,0:T(8,128)(2,1)} async-done(((bf16[1,64,4096]{2,1,0:T(8,128)(2,1)}), bf16[8,64,4096]{2,1,0:T(8,128)(2,1)}) %all-gather.3.cloned.1.call-update) | async-done | bytes 4194320 | tf_op jit(solution)/shard_map/all_gather | solution.py:99
  52.1 39.6 %all-gather.5.cloned.1.call-done.up_ref = bf16[8,64,4096]{2,1,0:T(8,128)(2,1)} async-done(((bf16[1,64,4096]{2,1,0:T(8,128)(2,1)}), bf16[8,64,4096]{2,1,0:T(8,128)(2,1)}) %all-gather.5.cloned.1.call-update) | async-done | bytes 4194320 | tf_op jit(solution)/shard_map/all_gather | solution.py:100
  91.7 14.6 %shard_map.86 = bf16[8,16,8448]{2,1,0:T(8,128)(2,1)S(1)} custom-call(bf16[16,4096]{1,0:T(8,128)(2,1)S(1)} %get-tuple-element.5.x_ref, bf16[16,4096]{1,0:T(8,128)(2,1)S(1)} %get-tuple-element.4.c_ref, s32[16,1]{1,0:T(8,128)S(1)} %copy.17.slot_ref, bf16[8,64,4096]{2,1,0:T(8,128)(2,1)} %all-gather.3.cloned.1.call-done.down_ref, ...), custom_call_target="tpu_custom_call" | custom-call | tf_op jit(solution)/shard_map/pallas_call | solution.py:71
  106.3 30.7 %all_to_all.15 = bf16[8,16,8448]{2,1,0:T(8,128)(2,1)S(1)} all-to-all(bf16[8,16,8448]{2,1,0:T(8,128)(2,1)S(1)} %shard_map.86), channel_id=1, replica_groups=mesh['section'=8,'dp'=64] {'section'}, dimensions={0} | all-to-all | bytes 4325376 | tf_op jit(solution)/shard_map/all_to_all | solution.py:105
  136.9 0.4 convolution_convert_fusion
  137.3 0.3 convolution_convert_fusion.1
  137.6 0.3 convolution_bitcast_fusion.2
  137.9 0.4 convolution_bitcast_fusion.1
  138.4 0.1 copy.19
  138.5 0.1 copy.20
  138.6 0.1 copy.21
  138.7 0.1 fusion.2
  138.8 0.0 copy-start.1
  138.8 0.0 copy-start.2
  138.8 1.1 pad_maximum_fusion
  139.9 13.4 %all-to-all-start.1 = ((bf16[64,64,128]{2,1,0:T(8,128)(2,1)}), bf16[64,64,128]{2,1,0:T(8,128)(2,1)S(1)}, u32[]{:S(2)}, u32[]{:S(2)}) async-start(bf16[64,64,128]{2,1,0:T(8,128)(2,1)} %pad_maximum_fusion), calls=%async_computation.1 | async-start | bytes 2097152 | tf_op jit(solution)/shard_map/all_to_all | solution.py:131
  153.3 0.2 select_reduce_fusion
  153.5 29.0 %all-to-all-done.1 = bf16[64,64,128]{2,1,0:T(8,128)(2,1)S(1)} async-done(((bf16[64,64,128]{2,1,0:T(8,128)(2,1)}), bf16[64,64,128]{2,1,0:T(8,128)(2,1)S(1)}, u32[]{:S(2)}, u32[]{:S(2)}) %all-to-all-start.1) | async-done | bytes 1048608 | tf_op jit(solution)/shard_map/all_to_all | solution.py:131
  182.5 0.3 reshape.41
  182.7 1.3 fusion.1
  184.0 0.1 copy.22
  184.1 25.3 %all_to_all.16 = bf16[64,32,128]{2,1,0:T(8,128)(2,1)S(1)} all-to-all(bf16[64,32,128]{2,1,0:T(8,128)(2,1)S(1)} %bitcast.33), channel_id=1, replica_groups=mesh['section'=8,'dp'=64] {'dp'}, dimensions={0} | all-to-all | bytes 1048576 | tf_op jit(solution)/shard_map/all_to_all | solution.py:141
  209.4 0.1 fusion.14
  209.6 0.9 squeeze.17
  210.5 0.9 squeeze.18
  (5 shorter events, 0.1 us)
Async XLA Ops:
  7.2 1.5 copy-start
  7.2 44.9 %all-gather.3.cloned.1.call-start = ((), (), s32[]{:S(2)}) async-start(), calls=%async_computation.3 | async-start | bytes 4718592 | tf_op jit(solution)/shard_map/all_gather | solution.py:99
  7.9 83.8 %all-gather.5.cloned.1.call-start = ((), (), s32[]{:S(2)}) async-start(), calls=%async_computation.4 | async-start | bytes 4718592 | tf_op jit(solution)/shard_map/all_gather | solution.py:100
  138.8 14.5 %copy-start.1 = (s32[64,2]{0,1:T(2,128)S(1)}, s32[64,2]{0,1:T(2,128)}, u32[]{:S(2)}) copy-start(s32[64,2]{0,1:T(2,128)} %param.10) | copy-start | bytes 1540
  138.8 14.5 %copy-start.2 = (s32[64]{0:T(128)S(1)}, s32[64]{0:T(128)}, u32[]{:S(2)}) copy-start(s32[64]{0:T(128)} %param.11) | copy-start | bytes 772
  139.9 42.6 %all-to-all-start.1 = ((bf16[64,64,128]{2,1,0:T(8,128)(2,1)}), bf16[64,64,128]{2,1,0:T(8,128)(2,1)S(1)}, u32[]{:S(2)}, u32[]{:S(2)}) async-start(bf16[64,64,128]{2,1,0:T(8,128)(2,1)} %pad_maximum_fusion), calls=%async_computation.1 | async-start | bytes 2097152 | tf_op jit(solution)/shard_map/all_to_all | solution.py:131
Sparse Core Ops, SparseCore 0:
  10.1 41.9 all-gather.2
  54.3 37.3 all-gather.4

commit v2 on v1

--- a/solution.py
+++ b/solution.py
@@ -9,14 +9,122 @@
 epsilon = 1e-06
 
 
-def relay_kernel(x_ref, c_ref, slot_ref, down_ref, up_ref, out_ref, hidden_ref, grad_ref):
-    sections, rank_columns, width = down_ref.shape
+MESH = pl.DeviceIdType.MESH
+
+
+def relay_kernel(
+    x_ref,
+    c_ref,
+    slot_ref,
+    down_ref,
+    up_ref,
+    normed_ref,
+    grads_ref,
+    weights,
+    hidden_ref,
+    grad_ref,
+    normed_out,
+    grads_out,
+    own_sem,
+    gather_send,
+    gather_recv,
+    rows_send,
+    rows_recv,
+):
+    sections, unused_pair, rank_columns, width = weights.shape
     rows = x_ref.shape[0]
     half = rank_columns // 2
+    me = lax.axis_index("section")
+    core = lax.rem(me, 2)
+    partner = me + 1 - 2 * core
+    right = lax.rem(me + 2, sections)
+    left = lax.rem(me + sections - 2, sections)
+    far = lax.rem(me + 4, sections)
+
+    barrier = pltpu.get_barrier_semaphore()
+    for step in range(1, sections):
+        pl.semaphore_signal(
+            barrier,
+            inc=1,
+            device_id={"section": lax.rem(me + step, sections)},
+            device_id_type=MESH,
+        )
+    pl.semaphore_wait(barrier, sections - 1)
+
+    def pass_on(number, src, owner, which, target):
+        return pltpu.make_async_remote_copy(
+            src_ref=src,
+            dst_ref=weights.at[owner, which],
+            send_sem=gather_send.at[number],
+            recv_sem=gather_recv.at[number],
+            device_id={"section": target},
+            device_id_type=MESH,
+        )
+
+    def forwarded(number, owner, which, target):
+        return pass_on(number, weights.at[owner, which], owner, which, target)
+
+    copies = [
+        pass_on(0, down_ref, me, 0, right),
+        pass_on(1, up_ref, me, 1, left),
+        pass_on(2, up_ref, me, 1, right),
+        pass_on(3, down_ref, me, 0, left),
+        pass_on(4, down_ref, me, 0, partner),
+        pass_on(5, up_ref, me, 1, partner),
+    ]
+    for copy in copies:
+        copy.start()
+    own = [
+        pltpu.make_async_copy(down_ref, weights.at[me, 0], own_sem.at[0]),
+        pltpu.make_async_copy(up_ref, weights.at[me, 1], own_sem.at[1]),
+    ]
+    for copy in own:
+        copy.start()
+
+    def send_on(number, owner, which, target):
+        copy = forwarded(number, owner, which, target)
+        copy.start()
+        copies.append(copy)
+
+    copies[0].wait_recv()
+    send_on(6, left, 0, right)
+    send_on(8, left, 0, partner)
+    copies[1].wait_recv()
+    send_on(7, right, 1, left)
+    send_on(9, right, 1, partner)
+    copies[2].wait_recv()
+    send_on(10, left, 1, partner)
+    copies[3].wait_recv()
+    send_on(11, right, 0, partner)
+    copies[6].wait_recv()
+    send_on(12, far, 0, partner)
+    copies[8].wait_recv()
+    send_on(13, far, 1, partner)
+
     column_slot = lax.broadcasted_iota(jnp.int32, (rows, rank_columns), 1) // half
     row_mask = slot_ref[...] == column_slot
     hidden_ref[0] = x_ref[...]
     grad_ref[...] = c_ref[...]
+    for copy in own:
+        copy.wait()
+    for place in (4, 5, 7, 9, 10, 11, 12, 13):
+        copies[place].wait_recv()
+
+    def rows_copy(kind, section, place):
+        source, target = ((normed_out, normed_ref), (grads_out, grads_ref))[kind]
+        return pltpu.make_async_remote_copy(
+            src_ref=source.at[section],
+            dst_ref=target.at[place],
+            send_sem=rows_send.at[kind, section],
+            recv_sem=rows_recv.at[kind, place],
+            device_id={"section": section},
+            device_id_type=MESH,
+        )
+
+    def send_rows(kind, section):
+        @pl.when(section != me)
+        def start():
+            rows_copy(kind, section, me).start()
 
     def norm_parts(section):
         hidden = hidden_ref[section].astype(jnp.float32)
@@ -26,17 +134,22 @@
     def forward(section, carried):
         hidden, inverse, unit = norm_parts(section)
         normed = unit.astype(jnp.bfloat16)
-        out_ref[section, :, 0:width] = normed
+        normed_out[section, :, 0:width] = normed
         rank = lax.dot_general(
             normed,
-            down_ref[section],
+            weights[section, 0],
             (((1,), (1,)), ((), ())),
             preferred_element_type=jnp.float32,
         )
         rank = jnp.where(row_mask, rank, 0.0).astype(jnp.bfloat16)
-        out_ref[section, :, 2 * width : 2 * width + rank_columns] = rank
-        update = jnp.dot(rank, up_ref[section], preferred_element_type=jnp.float32)
+        normed_out[section, :, width : width + rank_columns] = rank
+        update = jnp.dot(rank, weights[section, 1], preferred_element_type=jnp.float32)
         hidden_ref[section + 1] = (hidden + adapter_scale * update).astype(jnp.bfloat16)
+
+        @pl.when(section > 0)
+        def send_last():
+            send_rows(0, section - 1)
+
         return carried
 
     lax.fori_loop(0, sections, forward, 0)
@@ -45,40 +158,78 @@
         section = sections - 1 - step
         hidden, inverse, unit = norm_parts(section)
         grads = grad_ref[...]
-        out_ref[section, :, width : 2 * width] = grads
+        grads_out[section, :, 0:width] = grads
         rank_grads = adapter_scale * lax.dot_general(
             grads,
-            up_ref[section],
+            weights[section, 1],
             (((1,), (1,)), ((), ())),
             preferred_element_type=jnp.float32,
         )
         rank_grads = jnp.where(row_mask, rank_grads, 0.0).astype(jnp.bfloat16)
-        out_ref[section, :, 2 * width + 128 : 2 * width + 128 + rank_columns] = rank_grads
-        unit_grads = jnp.dot(rank_grads, down_ref[section], preferred_element_type=jnp.float32)
+        grads_out[section, :, width : width + rank_columns] = rank_grads
+        unit_grads = jnp.dot(
+            rank_grads, weights[section, 0], preferred_element_type=jnp.float32
+        )
         back = grads.astype(jnp.float32) + inverse * (
             unit_grads - unit * jnp.mean(unit_grads * unit, axis=-1, keepdims=True)
         )
         grad_ref[...] = back.astype(jnp.bfloat16)
+
+        @pl.when(step == 0)
+        def send_top():
+            send_rows(0, sections - 1)
+
+        @pl.when(step > 0)
+        def send_last():
+            send_rows(1, section + 1)
+
         return carried
 
     lax.fori_loop(0, sections, backward, 0)
-
-
-def relay(x, c, slot, down_every, up_every):
-    sections, rank_columns, width = down_every.shape
+    normed_ref[me] = normed_out[me]
+    grads_ref[me] = grads_out[me]
+    send_rows(1, 0)
+    for copy in copies:
+        copy.wait_send()
+
+    def finish(step, carried):
+        other = lax.rem(me + step, sections)
+        for kind in range(2):
+            copy = rows_copy(kind, other, other)
+            copy.wait_send()
+            copy.wait_recv()
+        return carried
+
+    lax.fori_loop(1, sections, finish, 0)
+
+
+def relay(x, c, slot, down_weight, up_weight):
+    sections = lax.axis_size("section")
+    rank_columns, width = down_weight.shape
     rows = x.shape[0]
     vmem = pl.BlockSpec(memory_space=pltpu.VMEM)
+    records = (sections, rows, width + 128)
     return pl.pallas_call(
         relay_kernel,
-        out_shape=jax.ShapeDtypeStruct((sections, rows, 2 * width + 256), jnp.bfloat16),
+        out_shape=[jax.ShapeDtypeStruct(records, jnp.bfloat16)] * 2,
         in_specs=[vmem] * 5,
-        out_specs=vmem,
+        out_specs=[vmem] * 2,
         scratch_shapes=[
+            pltpu.VMEM((sections, 2, rank_columns, width), jnp.bfloat16),
             pltpu.VMEM((sections + 1, rows, width), jnp.bfloat16),
             pltpu.VMEM((rows, width), jnp.bfloat16),
+            pltpu.VMEM(records, jnp.bfloat16),
+            pltpu.VMEM(records, jnp.bfloat16),
+            pltpu.SemaphoreType.DMA((2,)),
+            pltpu.SemaphoreType.DMA((14,)),
+            pltpu.SemaphoreType.DMA((14,)),
+            pltpu.SemaphoreType.DMA((2, sections)),
+            pltpu.SemaphoreType.DMA((2, sections)),
         ],
-        compiler_params=pltpu.CompilerParams(vmem_limit_bytes=48 * 1024 * 1024),
-    )(x, c, slot, down_every, up_every)
+        compiler_params=pltpu.CompilerParams(
+            collective_id=0, has_side_effects=True, vmem_limit_bytes=48 * 1024 * 1024
+        ),
+    )(x, c, slot, down_weight, up_weight)
 
 
 def body(
@@ -96,18 +247,18 @@
     slot_count = adapter_down_weight.shape[3]
     rank = adapter_down_weight.shape[4]
     rank_columns = slot_count * rank
-    down_every = lax.all_gather(adapter_down_weight.reshape(rank_columns, width), "section")
-    up_every = lax.all_gather(adapter_up_weight.reshape(rank_columns, width), "section")
+    down_weight = adapter_down_weight.reshape(rank_columns, width)
+    up_weight = adapter_up_weight.reshape(rank_columns, width)
     x = lax.dynamic_index_in_dim(inputs, section_index, 0, keepdims=False)
     c = lax.dynamic_index_in_dim(cotangent, section_index, 0, keepdims=False)
     slot = lax.dynamic_index_in_dim(row_adapter_slot, section_index, 0, keepdims=False)
-    packed = relay(x, c, slot[:, None], down_every, up_every)
-    packed = lax.all_to_all(packed, "section", split_axis=0, concat_axis=0, tiled=True)
-    packed = packed.reshape(micro_count * row_count, 2 * width + 256)
-    normed = packed[:, :width]
-    grads = packed[:, width : 2 * width]
-    rank_rows = packed[:, 2 * width : 2 * width + rank_columns]
-    rank_grads = packed[:, 2 * width + 128 : 2 * width + 128 + rank_columns]
+    normed, grads = relay(x, c, slot[:, None], down_weight, up_weight)
+    normed = normed.reshape(micro_count * row_count, width + 128)
+    grads = grads.reshape(micro_count * row_count, width + 128)
+    rank_rows = normed[:, width : width + rank_columns]
+    rank_grads = grads[:, width : width + rank_columns]
+    normed = normed[:, :width]
+    grads = grads[:, :width]
 
     def tile(rank_values, row_values):
         return jnp.concatenate(

time: 218 us -> 155 us (0.71)
  waiting for transfers between devices: 112 us -> 29.7 us
  Pallas kernels: 14.6 us -> 71.3 us
  blocking collectives: 56 us -> 25.9 us
  between operations: 14.2 us -> 0.77 us
  starting transfers between devices: 13.5 us -> 16.7 us
  local copies, waits for them, and re-layouts: 3.67 us -> 6.41 us
    all_gather x2 -> x0, waiting for transfers between devices: 81.9 us -> none  [the longest x1 42.3 us: body(): lax.all_gather(adapter_down_weight.reshape(rank_columns, width), 'section')]
    pallas_call x1, Pallas kernels: 14.6 us -> 71.3 us  [relay(): pl.pallas_call(relay_kernel, out_shape=[jax.ShapeDtypeStruct(records, jnp...]
    all_to_all x1 -> x0, blocking collectives: 30.7 us -> none  [body(): lax.all_to_all(packed, 'section', split_axis=0, concat_axis=0, tiled=True)]
    all_to_all x1, starting transfers between devices: 13.4 us -> 16.7 us  [body(): tiles = lax.all_to_all(tiles, 'dp', split_axis=0, concat_axis=0, tiled=True)]
    unnamed x10 -> x14, local copies, waits for them, and re-layouts: 0.42 us -> 3.17 us
  transfers between devices with their start and end apart: 3 -> 1, of which waited for: 3 -> 1; matrix products, arithmetic and copies ran while one was open for 1% -> 0% of each run, Pallas kernels for 0% -> 0%
where the time goes in v2:
time: 155 us
  Pallas kernels  71.3 us (46%)
  waiting for transfers between devices  29.7 us (19%)
  blocking collectives  25.9 us (17%)
  starting transfers between devices  16.7 us (11%)
  local copies, waits for them, and re-layouts  6.41 us (4%)
  matrix products  2.68 us (2%)
    pallas_call x1, Pallas kernels, relay(): pl.pallas_call(relay_kernel, out_shape=[jax.ShapeDtypeStruct(records, jnp...  71.3 us
    all_to_all x1, waiting for transfers between devices, body(): tiles = lax.all_to_all(tiles, 'dp', split_axis=0, concat_axis=0, tiled=True)  29.7 us
    all_to_all x1, blocking collectives, body(): final = lax.all_to_all(owned, 'dp', split_axis=0, concat_axis=0, tiled=True)  25.9 us
    all_to_all x1, starting transfers between devices, body(): tiles = lax.all_to_all(tiles, 'dp', split_axis=0, concat_axis=0, tiled=True)  16.7 us
    unnamed x14, local copies, waits for them, and re-layouts  3.17 us
  transfers between devices with their start and end apart: 1, of which 1 were waited for; matrix products, arithmetic and copies ran while one was open for 0% of the time, Pallas kernels for 0%

profile of v2, /device:TPU:8, one launch (start us, length us, event | category | flops | bytes accessed | tf_op | source)
XLA Modules:
  0.0 154.7 jit_solution(7504056924440744998)
XLA Ops:
  0.6 0.0 copy-start
  0.6 0.7 copy-done
  1.3 0.1 copy.14.slot_ref
  1.4 1.0 dynamic-slice_bitcast_fusion
  2.4 0.0 copy-start.1
  2.4 1.0 copy-done.1
  3.4 0.0 copy-start.2
  3.5 1.0 copy-done.2
  4.5 71.3 %shard_map.86 = (bf16[8,16,4224]{2,1,0:T(8,128)(2,1)S(1)}, bf16[8,16,4224]{2,1,0:T(8,128)(2,1)S(1)}) custom-call(bf16[16,4096]{1,0:T(8,128)(2,1)S(1)} %get-tuple-element.9.x_ref, bf16[16,4096]{1,0:T(8,128)(2,1)S(1)} %get-tuple-element.8.c_ref, s32[16,1]{1,0:T(8,128)S(1)} %copy.14.slot_ref, bf16[64,4096]{1,0:T(8,128)(2,1)S(1)} %bitcast.36, ...), custom_call_target="tpu_custom_call" | custom-call | tf_op jit(solution)/shard_map/pallas_call | solution.py:212
  75.8 0.4 convolution_convert_fusion
  76.1 0.3 convolution_convert_fusion.1
  76.5 0.3 convolution_bitcast_fusion.2
  76.8 0.4 convolution_bitcast_fusion.1
  77.2 0.1 copy.16
  77.3 0.1 copy.17
  77.4 0.1 copy.18
  77.5 0.1 fusion.2
  77.6 1.1 pad_maximum_fusion
  78.7 0.0 copy-start.3
  78.7 0.0 copy-start.4
  78.7 16.7 %all-to-all-start = ((bf16[64,64,128]{2,1,0:T(8,128)(2,1)}), bf16[64,64,128]{2,1,0:T(8,128)(2,1)S(1)}, u32[]{:S(2)}, u32[]{:S(2)}) async-start(bf16[64,64,128]{2,1,0:T(8,128)(2,1)} %pad_maximum_fusion), calls=%async_computation | async-start | bytes 2097152 | tf_op jit(solution)/shard_map/all_to_all | solution.py:282
  95.4 0.0 copy-done.3
  95.4 0.0 copy-done.4
  95.5 0.2 select_reduce_fusion
  95.6 29.7 %all-to-all-done = bf16[64,64,128]{2,1,0:T(8,128)(2,1)S(1)} async-done(((bf16[64,64,128]{2,1,0:T(8,128)(2,1)}), bf16[64,64,128]{2,1,0:T(8,128)(2,1)S(1)}, u32[]{:S(2)}, u32[]{:S(2)}) %all-to-all-start) | async-done | bytes 1048608 | tf_op jit(solution)/shard_map/all_to_all | solution.py:282
  125.3 0.3 reshape.53
  125.6 1.3 fusion.1
  126.9 0.1 copy.19
  127.0 25.9 %all_to_all.10 = bf16[64,32,128]{2,1,0:T(8,128)(2,1)S(1)} all-to-all(bf16[64,32,128]{2,1,0:T(8,128)(2,1)S(1)} %bitcast.40), channel_id=1, replica_groups=mesh['section'=8,'dp'=64] {'dp'}, dimensions={0} | all-to-all | bytes 1048576 | tf_op jit(solution)/shard_map/all_to_all | solution.py:292
  152.8 0.1 fusion.14
  153.0 0.9 squeeze.17
  153.9 0.9 squeeze.18
  (2 shorter events, 0.0 us)
Async XLA Ops:
  0.6 0.7 copy-start
  2.4 1.0 copy-start.1
  3.4 1.0 copy-start.2
  78.7 16.7 %copy-start.3 = (s32[64,2]{0,1:T(2,128)S(1)}, s32[64,2]{0,1:T(2,128)}, u32[]{:S(2)}) copy-start(s32[64,2]{0,1:T(2,128)} %param.10) | copy-start | bytes 1540
  78.7 16.7 %copy-start.4 = (s32[64]{0:T(128)S(1)}, s32[64]{0:T(128)}, u32[]{:S(2)}) copy-start(s32[64]{0:T(128)} %param.11) | copy-start | bytes 772
  78.7 46.6 %all-to-all-start = ((bf16[64,64,128]{2,1,0:T(8,128)(2,1)}), bf16[64,64,128]{2,1,0:T(8,128)(2,1)S(1)}, u32[]{:S(2)}, u32[]{:S(2)}) async-start(bf16[64,64,128]{2,1,0:T(8,128)(2,1)} %pad_maximum_fusion), calls=%async_computation | async-start | bytes 2097152 | tf_op jit(solution)/shard_map/all_to_all | solution.py:282

commit v3 on v2

--- a/solution.py
+++ b/solution.py
@@ -232,6 +232,109 @@
     )(x, c, slot, down_weight, up_weight)
 
 
+def owners_kernel(
+    tiles_ref, select_ref, out_ref, pieces_in, owned, own_sem, send_sem, recv_sem
+):
+    pieces = tiles_ref.shape[0]
+    slot_count = select_ref.shape[0]
+    lanes = tiles_ref.shape[1] // slot_count
+    side = 8
+    me = lax.axis_index("dp")
+    me_z, me_y = lax.div(me, side), lax.rem(me, side)
+
+    def peer(step):
+        z = lax.rem(me_z + lax.div(step, side), side)
+        y = lax.rem(me_y + lax.rem(step, side), side)
+        return z * side + y
+
+    barrier = pltpu.get_barrier_semaphore()
+
+    def greet(step, carried):
+        pl.semaphore_signal(
+            barrier, inc=1, device_id={"dp": peer(step)}, device_id_type=MESH
+        )
+        return carried
+
+    lax.fori_loop(1, pieces, greet, 0)
+    pl.semaphore_wait(barrier, pieces - 1)
+
+    def piece_copy(stage, other, place):
+        source, target = ((tiles_ref, pieces_in), (owned, out_ref))[stage]
+        return pltpu.make_async_remote_copy(
+            src_ref=source.at[other],
+            dst_ref=target.at[place],
+            send_sem=send_sem.at[stage, other],
+            recv_sem=recv_sem.at[stage, place],
+            device_id={"dp": other},
+            device_id_type=MESH,
+        )
+
+    def send(stage):
+        def one(step, carried):
+            piece_copy(stage, peer(step), me).start()
+            return carried
+
+        lax.fori_loop(1, pieces, one, 0)
+
+    def receive(stage):
+        def one(step, carried):
+            other = peer(step)
+            piece_copy(stage, other, other).wait_recv()
+            return carried
+
+        lax.fori_loop(1, pieces, one, 0)
+
+    send(0)
+    own = pltpu.make_async_copy(tiles_ref.at[me], pieces_in.at[me], own_sem.at[0])
+    own.start()
+    own.wait()
+    receive(0)
+    by_lanes = jnp.swapaxes(pieces_in[...], 0, 1)
+    sums = []
+    for lane in range(lanes):
+        total = None
+        for k in range(slot_count):
+            term = jnp.dot(
+                select_ref[k], by_lanes[k * lanes + lane], preferred_element_type=jnp.float32
+            )
+            total = term if total is None else total + term
+        sums.append(total.astype(jnp.bfloat16))
+    owned[...] = jnp.swapaxes(jnp.stack(sums), 0, 1)
+    send(1)
+    out_ref[me] = owned[me]
+    receive(1)
+
+    def finish(step, carried):
+        other = peer(step)
+        for stage in range(2):
+            piece_copy(stage, other, other).wait_send()
+        return carried
+
+    lax.fori_loop(1, pieces, finish, 0)
+
+
+def to_owners(tiles, select):
+    pieces, blocks, columns = tiles.shape
+    lanes = blocks // select.shape[0]
+    vmem = pl.BlockSpec(memory_space=pltpu.VMEM)
+    return pl.pallas_call(
+        owners_kernel,
+        out_shape=jax.ShapeDtypeStruct((pieces, lanes, columns), jnp.bfloat16),
+        in_specs=[vmem] * 2,
+        out_specs=vmem,
+        scratch_shapes=[
+            pltpu.VMEM((pieces, blocks, columns), jnp.bfloat16),
+            pltpu.VMEM((pieces, lanes, columns), jnp.bfloat16),
+            pltpu.SemaphoreType.DMA((1,)),
+            pltpu.SemaphoreType.DMA((2, pieces)),
+            pltpu.SemaphoreType.DMA((2, pieces)),
+        ],
+        compiler_params=pltpu.CompilerParams(
+            collective_id=1, has_side_effects=True, vmem_limit_bytes=32 * 1024 * 1024
+        ),
+    )(tiles, select)
+
+
 def body(
     inputs,
     cotangent,
@@ -279,17 +382,13 @@
     ).astype(jnp.bfloat16)
     lanes = width // 128
     tiles = tiles.reshape(pieces, slot_count * lanes, 128)
-    tiles = lax.all_to_all(tiles, "dp", split_axis=0, concat_axis=0, tiled=True)
-    tiles = tiles.reshape(pieces, slot_count, width)
     adapter_ids = jnp.arange(adapter_owner_device.shape[0], dtype=jnp.int32)
     owner_of = jnp.sum(
         jnp.where(deployed_adapter_ids[..., None] == adapter_ids, adapter_owner_device, 0), axis=-1
     )
     owner_ids = jnp.arange(pieces, dtype=jnp.int32)
-    select = (owner_of[None, :, :] == owner_ids[:, None, None]).astype(jnp.bfloat16)
-    owned = jnp.einsum("odk,dkx->ox", select, tiles, preferred_element_type=jnp.float32)
-    owned = owned.astype(jnp.bfloat16).reshape(pieces, lanes, 128)
-    final = lax.all_to_all(owned, "dp", split_axis=0, concat_axis=0, tiled=True)
+    select = (owner_of.T[:, None, :] == owner_ids[None, :, None]).astype(jnp.bfloat16)
+    final = to_owners(tiles, select)
     final = final.reshape(2, 1, 1, 1, rank, width).astype(jnp.float32)
     return (final[0], final[1])
 

time: 155 us -> 161 us (1.039)
  the two profiles are of different devices: /device:TPU:8 before, /device:TPU:16 now
where the time goes in v3:
time: 161 us
  Pallas kernels  152 us (94%)
  local copies, waits for them, and re-layouts  5.96 us (4%)
    pallas_call x1, Pallas kernels, to_owners(): pl.pallas_call(owners_kernel, out_shape=jax.ShapeDtypeStruct((pieces, lan...  80.8 us
    pallas_call x1, Pallas kernels, relay(): pl.pallas_call(relay_kernel, out_shape=[jax.ShapeDtypeStruct(records, jnp...  71.3 us

profile of v3, /device:TPU:16, one launch (start us, length us, event | category | flops | bytes accessed | tf_op | source)
XLA Modules:
  0.0 160.6 jit_solution(12251309791687056860)
XLA Ops:
  0.6 0.0 copy-start
  0.6 1.0 dynamic-slice_bitcast_fusion
  1.6 0.0 copy-done
  1.7 0.1 copy.11.slot_ref
  1.8 0.0 copy-start.1
  1.8 1.0 copy-done.1
  2.8 0.0 copy-start.2
  2.8 1.0 copy-done.2
  3.8 71.3 %shard_map.86 = (bf16[8,16,4224]{2,1,0:T(8,128)(2,1)S(1)}, bf16[8,16,4224]{2,1,0:T(8,128)(2,1)S(1)}) custom-call(bf16[16,4096]{1,0:T(8,128)(2,1)S(1)} %get-tuple-element.9.x_ref, bf16[16,4096]{1,0:T(8,128)(2,1)S(1)} %get-tuple-element.8.c_ref, s32[16,1]{1,0:T(8,128)S(1)} %copy.11.slot_ref, bf16[64,4096]{1,0:T(8,128)(2,1)S(1)} %bitcast.28, ...), custom_call_target="tpu_custom_call" | custom-call | tf_op jit(solution)/shard_map/pallas_call | solution.py:212
  75.1 0.4 convolution_convert_fusion
  75.5 0.3 convolution_convert_fusion.1
  75.8 0.1 copy.12
  76.0 0.3 convolution_bitcast_fusion.1
  76.3 0.1 copy.13
  76.4 0.4 convolution_bitcast_fusion
  76.8 0.1 copy.14
  76.9 0.1 fusion
  77.0 0.0 copy-start.3
  77.0 0.0 copy-start.4
  77.0 0.1 pad_maximum_fusion.tiles_ref
  77.1 0.6 copy-done.3
  77.7 0.0 copy-done.4
  77.7 0.2 select_reduce_fusion
  77.9 80.8 %shard_map.87 = bf16[64,32,128]{2,1,0:T(8,128)(2,1)S(1)} custom-call(bf16[64,64,128]{2,1,0:T(8,128)(2,1)S(1)} %pad_maximum_fusion.tiles_ref, bf16[2,64,64]{2,1,0:T(8,128)(2,1)S(1)} %fusion.5.select_ref), custom_call_target="tpu_custom_call" | custom-call | tf_op jit(solution)/shard_map/pallas_call | solution.py:320
  158.7 0.1 fusion.11
  158.8 0.9 squeeze.17
  159.7 0.9 squeeze.18
  (3 shorter events, 0.1 us)
Async XLA Ops:
  0.6 1.0 copy-start
  1.8 1.0 copy-start.1
  2.8 1.0 copy-start.2
  77.0 0.7 copy-start.3
  77.0 0.7 copy-start.4

commit v4 on v3

--- a/solution.py
+++ b/solution.py
@@ -242,9 +242,12 @@
     me = lax.axis_index("dp")
     me_z, me_y = lax.div(me, side), lax.rem(me, side)
 
+    turn = 1 - 2 * lax.rem(lax.axis_index("section"), 2)
+
     def peer(step):
-        z = lax.rem(me_z + lax.div(step, side), side)
-        y = lax.rem(me_y + lax.rem(step, side), side)
+        offset = lax.rem(step * 29, pieces)
+        z = lax.rem(me_z + turn * lax.div(offset, side) + side, side)
+        y = lax.rem(me_y + turn * lax.rem(offset, side) + side, side)
         return z * side + y
 
     barrier = pltpu.get_barrier_semaphore()

time: 161 us -> 145 us (0.901)
  the two profiles are of different devices: /device:TPU:16 before, /device:TPU:8 now
where the time goes in v4:
time: 145 us
  Pallas kernels  136 us (94%)
  local copies, waits for them, and re-layouts  5.96 us (4%)
    pallas_call x1, Pallas kernels, relay(): pl.pallas_call(relay_kernel, out_shape=[jax.ShapeDtypeStruct(records, jnp...  71.3 us
    pallas_call x1, Pallas kernels, to_owners(): pl.pallas_call(owners_kernel, out_shape=jax.ShapeDtypeStruct((pieces, lan...  64.9 us
    unnamed x13, local copies, waits for them, and re-layouts  2.97 us

profile of v4, /device:TPU:8, one launch (start us, length us, event | category | flops | bytes accessed | tf_op | source)
XLA Modules:
  0.0 144.7 jit_solution(17376033989123704909)
XLA Ops:
  0.6 0.0 copy-start
  0.6 1.0 dynamic-slice_bitcast_fusion
  1.6 0.0 copy-done
  1.7 0.1 copy.11.slot_ref
  1.8 0.0 copy-start.1
  1.8 1.0 copy-done.1
  2.8 0.0 copy-start.2
  2.8 1.0 copy-done.2
  3.8 71.3 %shard_map.86 = (bf16[8,16,4224]{2,1,0:T(8,128)(2,1)S(1)}, bf16[8,16,4224]{2,1,0:T(8,128)(2,1)S(1)}) custom-call(bf16[16,4096]{1,0:T(8,128)(2,1)S(1)} %get-tuple-element.9.x_ref, bf16[16,4096]{1,0:T(8,128)(2,1)S(1)} %get-tuple-element.8.c_ref, s32[16,1]{1,0:T(8,128)S(1)} %copy.11.slot_ref, bf16[64,4096]{1,0:T(8,128)(2,1)S(1)} %bitcast.28, ...), custom_call_target="tpu_custom_call" | custom-call | tf_op jit(solution)/shard_map/pallas_call | solution.py:212
  75.1 0.4 convolution_convert_fusion
  75.5 0.3 convolution_convert_fusion.1
  75.9 0.1 copy.12
  76.0 0.3 convolution_bitcast_fusion.1
  76.3 0.1 copy.13
  76.4 0.4 convolution_bitcast_fusion
  76.8 0.1 copy.14
  76.9 0.1 fusion
  77.0 0.0 copy-start.3
  77.0 0.0 copy-start.4
  77.0 0.1 pad_maximum_fusion.tiles_ref
  77.1 0.6 copy-done.3
  77.7 0.0 copy-done.4
  77.7 0.2 select_reduce_fusion
  77.9 64.9 %shard_map.87 = bf16[64,32,128]{2,1,0:T(8,128)(2,1)S(1)} custom-call(bf16[64,64,128]{2,1,0:T(8,128)(2,1)S(1)} %pad_maximum_fusion.tiles_ref, bf16[2,64,64]{2,1,0:T(8,128)(2,1)S(1)} %fusion.5.select_ref), custom_call_target="tpu_custom_call" | custom-call | tf_op jit(solution)/shard_map/pallas_call | solution.py:323
  142.8 0.1 fusion.11
  143.0 0.9 squeeze.17
  143.9 0.9 squeeze.18
  (3 shorter events, 0.1 us)
Async XLA Ops:
  0.6 1.0 copy-start
  1.8 1.0 copy-start.1
  2.8 1.0 copy-start.2
  77.0 0.7 copy-start.3
  77.0 0.7 copy-start.4

commit v5 on v2

--- a/solution.py
+++ b/solution.py
@@ -13,11 +13,13 @@
 
 
 def relay_kernel(
-    x_ref,
-    c_ref,
+    inputs_ref,
+    cotangent_ref,
     slot_ref,
     down_ref,
     up_ref,
+    select_ref,
+    out_ref,
     normed_ref,
     grads_ref,
     weights,
@@ -30,9 +32,14 @@
     gather_recv,
     rows_send,
     rows_recv,
+    tiles_ref,
+    pieces_in,
+    owned,
+    send_sem,
+    recv_sem,
 ):
     sections, unused_pair, rank_columns, width = weights.shape
-    rows = x_ref.shape[0]
+    rows = inputs_ref.shape[1]
     half = rank_columns // 2
     me = lax.axis_index("section")
     core = lax.rem(me, 2)
@@ -41,6 +48,21 @@
     left = lax.rem(me + sections - 2, sections)
     far = lax.rem(me + 4, sections)
 
+    pieces = lax.axis_size("dp")
+    slot_count = select_ref.shape[0]
+    lanes = width // 128
+    side = 8
+    me_dp = lax.axis_index("dp")
+    me_z, me_y = lax.div(me_dp, side), lax.rem(me_dp, side)
+
+    turn = 1 - 2 * core
+
+    def peer(step):
+        offset = lax.rem(step * 29, pieces)
+        z = lax.rem(me_z + turn * lax.div(offset, side) + side, side)
+        y = lax.rem(me_y + turn * lax.rem(offset, side) + side, side)
+        return z * side + y
+
     barrier = pltpu.get_barrier_semaphore()
     for step in range(1, sections):
         pl.semaphore_signal(
@@ -49,7 +71,15 @@
             device_id={"section": lax.rem(me + step, sections)},
             device_id_type=MESH,
         )
-    pl.semaphore_wait(barrier, sections - 1)
+
+    def greet(step, carried):
+        pl.semaphore_signal(
+            barrier, inc=1, device_id={"dp": peer(step)}, device_id_type=MESH
+        )
+        return carried
+
+    lax.fori_loop(1, pieces, greet, 0)
+    pl.semaphore_wait(barrier, sections - 1 + pieces - 1)
 
     def pass_on(number, src, owner, which, target):
         return pltpu.make_async_remote_copy(
@@ -77,6 +107,8 @@
     own = [
         pltpu.make_async_copy(down_ref, weights.at[me, 0], own_sem.at[0]),
         pltpu.make_async_copy(up_ref, weights.at[me, 1], own_sem.at[1]),
+        pltpu.make_async_copy(inputs_ref.at[me], hidden_ref.at[0], own_sem.at[2]),
+        pltpu.make_async_copy(cotangent_ref.at[me], grad_ref, own_sem.at[3]),
     ]
     for copy in own:
         copy.start()
@@ -103,8 +135,6 @@
 
     column_slot = lax.broadcasted_iota(jnp.int32, (rows, rank_columns), 1) // half
     row_mask = slot_ref[...] == column_slot
-    hidden_ref[0] = x_ref[...]
-    grad_ref[...] = c_ref[...]
     for copy in own:
         copy.wait()
     for place in (4, 5, 7, 9, 10, 11, 12, 13):
@@ -202,34 +232,119 @@
 
     lax.fori_loop(1, sections, finish, 0)
 
-
-def relay(x, c, slot, down_weight, up_weight):
+    tiles = []
+    for rank_from, rows_from in ((grads_ref, normed_ref), (normed_ref, grads_ref)):
+        rank_values = rank_from[:, :, width : width + rank_columns].reshape(-1, rank_columns)
+        row_values = rows_from[:, :, 0:width].reshape(-1, width)
+        tile = lax.dot_general(
+            rank_values,
+            row_values,
+            (((0,), (0,)), ((), ())),
+            preferred_element_type=jnp.float32,
+        )
+        if rank_from is normed_ref:
+            tile = adapter_scale * tile
+        tile = tile.astype(jnp.bfloat16)
+        blocks = [
+            tile[k * half : (k + 1) * half, 128 * lane : 128 * (lane + 1)]
+            for k in range(slot_count)
+            for lane in range(lanes)
+        ]
+        tiles.append(jnp.swapaxes(jnp.stack(blocks), 0, 1))
+    tiles_ref[0:half] = tiles[0]
+    tiles_ref[half : 2 * half] = tiles[1]
+
+    def piece_copy(stage, other, place):
+        source, target = ((tiles_ref, pieces_in), (owned, out_ref))[stage]
+        return pltpu.make_async_remote_copy(
+            src_ref=source.at[other],
+            dst_ref=target.at[place],
+            send_sem=send_sem.at[stage, other],
+            recv_sem=recv_sem.at[stage, place],
+            device_id={"dp": other},
+            device_id_type=MESH,
+        )
+
+    def send(stage):
+        def one(step, carried):
+            piece_copy(stage, peer(step), me_dp).start()
+            return carried
+
+        lax.fori_loop(1, pieces, one, 0)
+
+    def receive(stage):
+        def one(step, carried):
+            other = peer(step)
+            piece_copy(stage, other, other).wait_recv()
+            return carried
+
+        lax.fori_loop(1, pieces, one, 0)
+
+    send(0)
+    pieces_in[me_dp] = tiles_ref[me_dp]
+    receive(0)
+    by_lanes = jnp.swapaxes(pieces_in[...], 0, 1)
+    sums = []
+    for lane in range(lanes):
+        total = None
+        for k in range(slot_count):
+            term = jnp.dot(
+                select_ref[k], by_lanes[k * lanes + lane], preferred_element_type=jnp.float32
+            )
+            total = term if total is None else total + term
+        sums.append(total.astype(jnp.bfloat16))
+    owned[...] = jnp.swapaxes(jnp.stack(sums), 0, 1)
+    send(1)
+    out_ref[me_dp] = owned[me_dp]
+    receive(1)
+
+    def drain(step, carried):
+        other = peer(step)
+        for stage in range(2):
+            piece_copy(stage, other, other).wait_send()
+        return carried
+
+    lax.fori_loop(1, pieces, drain, 0)
+
+
+def relay(inputs, cotangent, slot, down_weight, up_weight, select):
     sections = lax.axis_size("section")
+    pieces = lax.axis_size("dp")
     rank_columns, width = down_weight.shape
-    rows = x.shape[0]
+    rows = inputs.shape[1]
+    slot_count = select.shape[0]
+    lanes = width // 128
     vmem = pl.BlockSpec(memory_space=pltpu.VMEM)
+    anywhere = pl.BlockSpec(memory_space=pl.ANY)
     records = (sections, rows, width + 128)
     return pl.pallas_call(
         relay_kernel,
-        out_shape=[jax.ShapeDtypeStruct(records, jnp.bfloat16)] * 2,
-        in_specs=[vmem] * 5,
-        out_specs=[vmem] * 2,
+        out_shape=jax.ShapeDtypeStruct((pieces, lanes, 128), jnp.bfloat16),
+        in_specs=[anywhere, anywhere, vmem, anywhere, anywhere, vmem],
+        out_specs=vmem,
         scratch_shapes=[
+            pltpu.VMEM(records, jnp.bfloat16),
+            pltpu.VMEM(records, jnp.bfloat16),
             pltpu.VMEM((sections, 2, rank_columns, width), jnp.bfloat16),
             pltpu.VMEM((sections + 1, rows, width), jnp.bfloat16),
             pltpu.VMEM((rows, width), jnp.bfloat16),
             pltpu.VMEM(records, jnp.bfloat16),
             pltpu.VMEM(records, jnp.bfloat16),
-            pltpu.SemaphoreType.DMA((2,)),
+            pltpu.SemaphoreType.DMA((4,)),
             pltpu.SemaphoreType.DMA((14,)),
             pltpu.SemaphoreType.DMA((14,)),
             pltpu.SemaphoreType.DMA((2, sections)),
             pltpu.SemaphoreType.DMA((2, sections)),
+            pltpu.VMEM((pieces, slot_count * lanes, 128), jnp.bfloat16),
+            pltpu.VMEM((pieces, slot_count * lanes, 128), jnp.bfloat16),
+            pltpu.VMEM((pieces, lanes, 128), jnp.bfloat16),
+            pltpu.SemaphoreType.DMA((2, pieces)),
+            pltpu.SemaphoreType.DMA((2, pieces)),
         ],
         compiler_params=pltpu.CompilerParams(
-            collective_id=0, has_side_effects=True, vmem_limit_bytes=48 * 1024 * 1024
+            collective_id=0, has_side_effects=True, vmem_limit_bytes=56 * 1024 * 1024
         ),
-    )(x, c, slot, down_weight, up_weight)
+    )(inputs, cotangent, slot, down_weight, up_weight, select)
 
 
 def body(
@@ -249,47 +364,14 @@
     rank_columns = slot_count * rank
     down_weight = adapter_down_weight.reshape(rank_columns, width)
     up_weight = adapter_up_weight.reshape(rank_columns, width)
-    x = lax.dynamic_index_in_dim(inputs, section_index, 0, keepdims=False)
-    c = lax.dynamic_index_in_dim(cotangent, section_index, 0, keepdims=False)
     slot = lax.dynamic_index_in_dim(row_adapter_slot, section_index, 0, keepdims=False)
-    normed, grads = relay(x, c, slot[:, None], down_weight, up_weight)
-    normed = normed.reshape(micro_count * row_count, width + 128)
-    grads = grads.reshape(micro_count * row_count, width + 128)
-    rank_rows = normed[:, width : width + rank_columns]
-    rank_grads = grads[:, width : width + rank_columns]
-    normed = normed[:, :width]
-    grads = grads[:, :width]
-
-    def tile(rank_values, row_values):
-        return jnp.concatenate(
-            [
-                lax.dot_general(
-                    rank_values[:, k * rank : (k + 1) * rank],
-                    row_values,
-                    (((0,), (0,)), ((), ())),
-                    preferred_element_type=jnp.float32,
-                )
-                for k in range(slot_count)
-            ],
-            axis=-1,
-        )
-
-    tiles = jnp.concatenate(
-        [tile(rank_grads, normed), adapter_scale * tile(rank_rows, grads)], axis=0
-    ).astype(jnp.bfloat16)
-    lanes = width // 128
-    tiles = tiles.reshape(pieces, slot_count * lanes, 128)
-    tiles = lax.all_to_all(tiles, "dp", split_axis=0, concat_axis=0, tiled=True)
-    tiles = tiles.reshape(pieces, slot_count, width)
     adapter_ids = jnp.arange(adapter_owner_device.shape[0], dtype=jnp.int32)
     owner_of = jnp.sum(
         jnp.where(deployed_adapter_ids[..., None] == adapter_ids, adapter_owner_device, 0), axis=-1
     )
     owner_ids = jnp.arange(pieces, dtype=jnp.int32)
-    select = (owner_of[None, :, :] == owner_ids[:, None, None]).astype(jnp.bfloat16)
-    owned = jnp.einsum("odk,dkx->ox", select, tiles, preferred_element_type=jnp.float32)
-    owned = owned.astype(jnp.bfloat16).reshape(pieces, lanes, 128)
-    final = lax.all_to_all(owned, "dp", split_axis=0, concat_axis=0, tiled=True)
+    select = (owner_of.T[:, None, :] == owner_ids[None, :, None]).astype(jnp.bfloat16)
+    final = relay(inputs, cotangent, slot[:, None], down_weight, up_weight, select)
     final = final.reshape(2, 1, 1, 1, rank, width).astype(jnp.float32)
     return (final[0], final[1])
 

time: 155 us -> 142 us (0.916)
  Pallas kernels: 71.3 us -> 135 us
  waiting for transfers between devices: 29.7 us -> 0 us
  blocking collectives: 25.9 us -> 0 us
  starting transfers between devices: 16.7 us -> 0 us
  matrix products: 2.68 us -> 0 us
    pallas_call x1, Pallas kernels: 71.3 us -> 135 us  [relay(): pl.pallas_call(relay_kernel, out_shape=jax.ShapeDtypeStruct((pieces, lane...]
    all_to_all x1 -> x0, waiting for transfers between devices: 29.7 us -> none  [body(): tiles = lax.all_to_all(tiles, 'dp', split_axis=0, concat_axis=0, tiled=True)]
    all_to_all x1 -> x0, blocking collectives: 25.9 us -> none  [body(): final = lax.all_to_all(owned, 'dp', split_axis=0, concat_axis=0, tiled=True)]
    all_to_all x1 -> x0, starting transfers between devices: 16.7 us -> none  [body(): tiles = lax.all_to_all(tiles, 'dp', split_axis=0, concat_axis=0, tiled=True)]
    dot_general x5 -> x0, matrix products: 2.68 us -> none  [the longest x4 1.37 us: tile(): lax.dot_general(rank_values[:, k * rank:(k + 1) * rank], row_values, (((0...]
    unnamed x14 -> x6, local copies, waits for them, and re-layouts: 3.17 us -> 1.35 us
  transfers between devices with their start and end apart: 1 -> 0, of which waited for: 1 -> 0; matrix products, arithmetic and copies ran while one was open for 0% -> 0% of each run, Pallas kernels for 0% -> 0%
where the time goes in v5:
time: 142 us
  Pallas kernels  135 us (95%)
  local copies, waits for them, and re-layouts  4.98 us (4%)
    pallas_call x1, Pallas kernels, relay(): pl.pallas_call(relay_kernel, out_shape=jax.ShapeDtypeStruct((pieces, lane...  135 us

profile of v5, /device:TPU:8, one launch (start us, length us, event | category | flops | bytes accessed | tf_op | source)
XLA Modules:
  0.0 141.9 jit_solution(15601473569837132590)
XLA Ops:
  0.6 0.0 copy-start
  0.6 0.7 copy-done
  1.3 0.0 copy-start.1
  1.3 0.0 copy-start.2
  1.3 0.7 copy-done.1
  2.0 0.0 copy-done.2
  2.0 0.2 select_reduce_fusion
  2.2 0.7 copy.11.slot_ref
  2.9 0.6 fusion.select_ref
  3.5 135.5 %shard_map.86 = bf16[64,32,128]{2,1,0:T(8,128)(2,1)} custom-call(bf16[8,16,4096]{2,1,0:T(8,128)(2,1)} %inputs_ref.1, bf16[8,16,4096]{2,1,0:T(8,128)(2,1)} %cotangent_ref.1, s32[16,1]{1,0:T(8,128)} %copy.11.slot_ref, bf16[64,4096]{1,0:T(8,128)(2,1)} %bitcast.5, bf16[64,4096]{1,0:T(8,128)(2,1)} %bitcast.6, bf16[2,64,64]{2,1,0:T(8,128)(2,1)} %fusion.select_ref), custom_call_target="tpu_custom_call" | custom-call | tf_op jit(solution)/shard_map/pallas_call | solution.py:320
  139.0 1.2 fusion.1
  140.1 0.9 squeeze.9
  141.0 0.9 squeeze.8
  (1 shorter events, 0.0 us)
Async XLA Ops:
  0.6 0.7 copy-start
  1.3 0.7 copy-start.1
  1.3 0.7 copy-start.2

commit v6 on v5

--- a/solution.py
+++ b/solution.py
@@ -37,6 +37,9 @@
     owned,
     send_sem,
     recv_sem,
+    relayed,
+    relay_send,
+    relay_recv,
 ):
     sections, unused_pair, rank_columns, width = weights.shape
     rows = inputs_ref.shape[1]
@@ -151,9 +154,43 @@
             device_id_type=MESH,
         )
 
+    def to_left(section):
+        which = lax.rem(section, 2)
+        return pltpu.make_async_remote_copy(
+            src_ref=normed_out.at[section],
+            dst_ref=relayed.at[which],
+            send_sem=rows_send.at[0, section],
+            recv_sem=relay_recv.at[which],
+            device_id={"section": left},
+            device_id_type=MESH,
+        )
+
+    def from_right(which):
+        return pltpu.make_async_remote_copy(
+            src_ref=relayed.at[which],
+            dst_ref=normed_ref.at[right],
+            send_sem=relay_send.at[which],
+            recv_sem=rows_recv.at[0, right],
+            device_id={"section": left - core + which},
+            device_id_type=MESH,
+        )
+
     def send_rows(kind, section):
-        @pl.when(section != me)
-        def start():
+        if kind == 1:
+
+            @pl.when(section != me)
+            def start():
+                rows_copy(kind, section, me).start()
+
+            return
+        opposite = lax.div(section, 2) == lax.div(far, 2)
+
+        @pl.when(opposite)
+        def start_left():
+            to_left(section).start()
+
+        @pl.when(jnp.logical_not(opposite) & (section != me))
+        def start_direct():
             rows_copy(kind, section, me).start()
 
     def norm_parts(section):
@@ -213,6 +250,12 @@
         def send_last():
             send_rows(1, section + 1)
 
+        @pl.when(step == 5)
+        def send_relayed():
+            for which in range(2):
+                to_left(which).wait_recv()
+                from_right(which).start()
+
         return carried
 
     lax.fori_loop(0, sections, backward, 0)
@@ -231,6 +274,8 @@
         return carried
 
     lax.fori_loop(1, sections, finish, 0)
+    for which in range(2):
+        from_right(which).wait_send()
 
     tiles = []
     for rank_from, rows_from in ((grads_ref, normed_ref), (normed_ref, grads_ref)):
@@ -340,6 +385,9 @@
             pltpu.VMEM((pieces, lanes, 128), jnp.bfloat16),
             pltpu.SemaphoreType.DMA((2, pieces)),
             pltpu.SemaphoreType.DMA((2, pieces)),
+            pltpu.VMEM((2, rows, width + 128), jnp.bfloat16),
+            pltpu.SemaphoreType.DMA((2,)),
+            pltpu.SemaphoreType.DMA((2,)),
         ],
         compiler_params=pltpu.CompilerParams(
             collective_id=0, has_side_effects=True, vmem_limit_bytes=56 * 1024 * 1024

time: 142 us -> 147 us (1.035)
  Pallas kernels: 135 us -> 140 us
    pallas_call x1, Pallas kernels: 135 us -> 140 us  [relay(): pl.pallas_call(relay_kernel, out_shape=jax.ShapeDtypeStruct((pieces, lane...]
where the time goes in v6:
time: 147 us; the launch traced here: 146 us
  Pallas kernels  140 us (95%)
  local copies, waits for them, and re-layouts  4.98 us (3%)
    pallas_call x1, Pallas kernels, relay(): pl.pallas_call(relay_kernel, out_shape=jax.ShapeDtypeStruct((pieces, lane...  140 us

profile of v6, /device:TPU:8, one launch (start us, length us, event | category | flops | bytes accessed | tf_op | source)
XLA Modules:
  0.0 146.3 jit_solution(3932983896458104570)
XLA Ops:
  0.6 0.0 copy-start
  0.6 0.7 copy-done
  1.3 0.0 copy-start.1
  1.3 0.0 copy-start.2
  1.3 0.7 copy-done.1
  2.0 0.0 copy-done.2
  2.0 0.2 select_reduce_fusion
  2.2 0.7 copy.11.slot_ref
  2.9 0.6 fusion.select_ref
  3.5 139.9 %shard_map.86 = bf16[64,32,128]{2,1,0:T(8,128)(2,1)} custom-call(bf16[8,16,4096]{2,1,0:T(8,128)(2,1)} %inputs_ref.1, bf16[8,16,4096]{2,1,0:T(8,128)(2,1)} %cotangent_ref.1, s32[16,1]{1,0:T(8,128)} %copy.11.slot_ref, bf16[64,4096]{1,0:T(8,128)(2,1)} %bitcast.5, bf16[64,4096]{1,0:T(8,128)(2,1)} %bitcast.6, bf16[2,64,64]{2,1,0:T(8,128)(2,1)} %fusion.select_ref), custom_call_target="tpu_custom_call" | custom-call | tf_op jit(solution)/shard_map/pallas_call | solution.py:365
  143.4 1.2 fusion.1
  144.6 0.9 squeeze.9
  145.5 0.9 squeeze.8
  (1 shorter events, 0.0 us)
Async XLA Ops:
  0.6 0.7 copy-start
  1.3 0.7 copy-start.1
  1.3 0.7 copy-start.2

commit v7 on v5

--- a/solution.py
+++ b/solution.py
@@ -19,7 +19,8 @@
     down_ref,
     up_ref,
     select_ref,
-    out_ref,
+    grad_down_ref,
+    grad_up_ref,
     normed_ref,
     grads_ref,
     weights,
@@ -35,6 +36,7 @@
     tiles_ref,
     pieces_in,
     owned,
+    out_ref,
     send_sem,
     recv_sem,
 ):
@@ -297,6 +299,11 @@
     send(1)
     out_ref[me_dp] = owned[me_dp]
     receive(1)
+    last = jnp.swapaxes(out_ref[...], 0, 1)
+    for lane in range(lanes):
+        columns = slice(128 * lane, 128 * (lane + 1))
+        grad_down_ref[:, columns] = last[lane, 0:half].astype(jnp.float32)
+        grad_up_ref[:, columns] = last[lane, half : 2 * half].astype(jnp.float32)
 
     def drain(step, carried):
         other = peer(step)
@@ -319,9 +326,9 @@
     records = (sections, rows, width + 128)
     return pl.pallas_call(
         relay_kernel,
-        out_shape=jax.ShapeDtypeStruct((pieces, lanes, 128), jnp.bfloat16),
+        out_shape=[jax.ShapeDtypeStruct((pieces // 2, width), jnp.float32)] * 2,
         in_specs=[anywhere, anywhere, vmem, anywhere, anywhere, vmem],
-        out_specs=vmem,
+        out_specs=[vmem] * 2,
         scratch_shapes=[
             pltpu.VMEM(records, jnp.bfloat16),
             pltpu.VMEM(records, jnp.bfloat16),
@@ -337,6 +344,7 @@
             pltpu.SemaphoreType.DMA((2, sections)),
             pltpu.VMEM((pieces, slot_count * lanes, 128), jnp.bfloat16),
             pltpu.VMEM((pieces, slot_count * lanes, 128), jnp.bfloat16),
+            pltpu.VMEM((pieces, lanes, 128), jnp.bfloat16),
             pltpu.VMEM((pieces, lanes, 128), jnp.bfloat16),
             pltpu.SemaphoreType.DMA((2, pieces)),
             pltpu.SemaphoreType.DMA((2, pieces)),
@@ -371,9 +379,11 @@
     )
     owner_ids = jnp.arange(pieces, dtype=jnp.int32)
     select = (owner_of.T[:, None, :] == owner_ids[None, :, None]).astype(jnp.bfloat16)
-    final = relay(inputs, cotangent, slot[:, None], down_weight, up_weight, select)
-    final = final.reshape(2, 1, 1, 1, rank, width).astype(jnp.float32)
-    return (final[0], final[1])
+    grad_down, grad_up = relay(inputs, cotangent, slot[:, None], down_weight, up_weight, select)
+    return (
+        grad_down.reshape(1, 1, 1, rank, width),
+        grad_up.reshape(1, 1, 1, rank, width),
+    )
 
 
 def solution(mesh):

time: 142 us -> 142 us (level)
    unnamed x6 -> x10, local copies, waits for them, and re-layouts: 1.35 us -> 4.08 us
    squeeze x2 -> x0, local copies, waits for them, and re-layouts: 1.78 us -> none  [body(): return (final[0], final[1])]
where the time goes in v7:
time: 142 us
  Pallas kernels  136 us (96%)
  local copies, waits for them, and re-layouts  4.77 us (3%)
    pallas_call x1, Pallas kernels, relay(): pl.pallas_call(relay_kernel, out_shape=[jax.ShapeDtypeStruct((pieces // 2...  136 us
    unnamed x10, local copies, waits for them, and re-layouts  4.08 us

profile of v7, /device:TPU:8, one launch (start us, length us, event | category | flops | bytes accessed | tf_op | source)
XLA Modules:
  0.0 142.0 jit_solution(13018827871204011053)
XLA Ops:
  0.6 0.0 copy-start
  0.6 0.7 copy-done
  1.3 0.0 copy-start.2
  1.3 0.0 copy-start.3
  1.3 0.7 copy-done.2
  2.0 0.0 copy-done.3
  2.0 0.2 select_reduce_fusion
  2.2 0.7 copy.11.slot_ref
  2.9 0.6 fusion.select_ref
  3.5 135.8 %shard_map.86 = (f32[32,4096]{1,0:T(8,128)}, f32[32,4096]{1,0:T(8,128)}) custom-call(bf16[8,16,4096]{2,1,0:T(8,128)(2,1)} %inputs_ref.1, bf16[8,16,4096]{2,1,0:T(8,128)(2,1)} %cotangent_ref.1, s32[16,1]{1,0:T(8,128)} %copy.11.slot_ref, bf16[64,4096]{1,0:T(8,128)(2,1)} %bitcast.7, bf16[64,4096]{1,0:T(8,128)(2,1)} %bitcast.8, bf16[2,64,64]{2,1,0:T(8,128)(2,1)} %fusion.select_ref), custom_call_target="tpu_custom_call" | custom-call | tf_op jit(solution)/shard_map/pallas_call | solution.py:327
  139.3 0.0 copy-start.1
  139.3 1.9 %copy.14 = f32[1,1,1,32,4096]{4,3,2,1,0:T(8,128)} copy(f32[1,1,1,32,4096]{4,3,2,1,0:T(8,128)} %bitcast.10) | data formatting | bytes 1048576
  141.2 0.0 copy-done.1
  141.2 0.8 copy.15
  (1 shorter events, 0.0 us)
Async XLA Ops:
  0.6 0.7 copy-start
  1.3 0.7 copy-start.2
  1.3 0.7 copy-start.3
  139.3 1.9 %copy-start.1 = (f32[32,4096]{1,0:T(8,128)S(1)}, f32[32,4096]{1,0:T(8,128)}, u32[]{:S(2)}) copy-start(f32[32,4096]{1,0:T(8,128)} %get-tuple-element.5) | copy-start | bytes 1572868
